TPU v7x, 32 devices: a whole 2x2x4 slice. The times are simulated.
32 devices in a mesh: seq: 4 (over y, x), dp: 4 (over z), enc: 2 (over core).
Axes of the slice: x: 2, y: 2, z: 4, core: 2. Of those that a mesh axis runs over, the one named last changes fastest.
Arguments:
- lm_grad: bfloat16 [4, 4, 192, 1152], P('dp', 'enc', 'seq'), may hold values from -6 to 6
- image_tokens: int32 [4, 4, 4], P('dp'), may hold values from 1 to 15, as said below
- image_offset: int32 [4, 4, 4], P('dp'), may hold values from 0 to 47, as said below
- image_owner: int32 [4, 4, 4], P('dp'), may hold values from 0 to 3, as said below
- mlp_input: bfloat16 [4, 4, 240, 1152], P('dp', None, 'seq'), may hold values from -36 to 36
- layer_output: bfloat16 [4, 4, 240, 1152], P('dp', 'enc', 'seq'), may hold values from -36 to 36
- pre_gain: float32 [1152], replicated, may hold values from 0.5 to 1.5
- pre_bias: float32 [1152], replicated, may hold values from -3 to 3
- fc1_weight: bfloat16 [1152, 4304], P(None, 'enc'), may hold values from -0.1875 to 0.1875
- fc1_bias: float32 [4304], P('enc'), may hold values from -3 to 3
- fc2_weight: bfloat16 [4304, 1152], P('enc'), may hold values from -0.09375 to 0.09375
- post_gain: float32 [1152], replicated, may hold values from 0.5 to 1.5
- post_bias: float32 [1152], replicated, may hold values from -3 to 3
- merge_gain: float32 [1152], replicated, may hold values from 0.5 to 1.5
Outputs:
- act_grad: bfloat16 [4, 4, 240, 1152], P('dp', 'enc', 'seq')
- norm_grads: float32 [6, 1152], replicated
- fc1_bias_grad: float32 [4304], replicated
Inputs may be any that keep to these rules, and one draw needn't show every extreme that they name: `image_tokens`: the 4 images of one LM shard have token counts that sum to 48, and one of them has 15. `image_offset`: the images of one LM shard lie back to back over its 48 rows, in some order; each entry is an image's first row in its shard. Images are placed round-robin by their index j in a shard: image_owner[r, q, j] = (q + image_owner[r, 0, j]) mod 4, with the 4 values image_owner[r, 0, j] different. So each encoder chip owns exactly 4 images of its replica, the visual tokens owned by one chip number at most 60, and some chip owns exactly 60.
All inputs are finite; a program needn't handle non-finite values.
Results may differ from a plain program's by a relative error of at most 0.005.
Values may be sent and summed in bfloat16 or wider, within the bound.
A program may use at most 64 MiB of HBM per device.

v0:
```python
import math

import jax
import jax.numpy as jnp
from jax import lax
from jax.sharding import PartitionSpec as P

D = 1152
FF = 4304
PATCH_GROUP = 4
ROWS_DEV = 48
CAP_TOK = 60


EPSILON = 1e-06
SLOPE_K = math.sqrt(2.0 / math.pi)
CUBIC = 0.044715


def layer_norm(values):
    row_mean = jnp.mean(values, axis=-1, keepdims=True)
    centred = values - row_mean
    return centred * lax.rsqrt(jnp.mean(centred * centred, axis=-1, keepdims=True) + EPSILON)


def rms_norm(values):
    return values * lax.rsqrt(jnp.mean(values * values, axis=-1, keepdims=True) + EPSILON)


def gelu_slope(pre_act):
    inner_arg = SLOPE_K * (pre_act + CUBIC * pre_act * pre_act * pre_act)
    tangent = jnp.tanh(inner_arg)
    return 0.5 * (1.0 + tangent) + 0.5 * pre_act * (1.0 - tangent * tangent) * SLOPE_K * (
        1.0 + 3.0 * CUBIC * pre_act * pre_act
    )


def head_back(incoming, layer_rows, merge_gain, post_gain, post_bias):

    def merge_head(row_values, merge_scale, post_scale, post_shift):
        return rms_norm(layer_norm(row_values) * post_scale + post_shift) * merge_scale

    _, pullback = jax.vjp(
        merge_head, layer_rows.astype(jnp.float32), merge_gain, post_gain, post_bias
    )
    return pullback(incoming.astype(jnp.float32))


def pre_back(input_rows, pre_gain, pre_bias, upstream):

    def prenorm(row_values, scale_vec, shift_vec):
        return layer_norm(row_values) * scale_vec + shift_vec

    _, pullback = jax.vjp(prenorm, input_rows.astype(jnp.float32), pre_gain, pre_bias)
    return pullback(upstream)


def slot_source(lengths, offsets, owners, chip_index):
    shard_count = lengths.shape[0]
    is_mine = owners == chip_index
    my_len = jnp.sum(jnp.where(is_mine, lengths, 0), axis=1)
    my_off = jnp.sum(jnp.where(is_mine, offsets, 0), axis=1)
    slot_first = jnp.cumsum(my_len) - my_len
    slot_ids = jnp.arange(CAP_TOK, dtype=jnp.int32)
    inside = (slot_ids[:, None] >= slot_first[None, :]) & (
        slot_ids[:, None] < (slot_first + my_len)[None, :]
    )
    live_slot = jnp.any(inside, axis=1)
    shard_ids = jnp.arange(shard_count, dtype=jnp.int32)
    source = jnp.sum(jnp.where(inside, shard_ids[None, :], 0), axis=1)
    token_index = slot_ids - jnp.sum(jnp.where(inside, slot_first[None, :], 0), axis=1)
    shard_row = jnp.sum(jnp.where(inside, my_off[None, :], 0), axis=1) + token_index
    return (live_slot, source, token_index, shard_row)


def body(
    lm_grad,
    image_tokens,
    image_offset,
    image_owner,
    mlp_input,
    layer_output,
    pre_gain,
    pre_bias,
    fc1_weight,
    fc1_bias,
    fc2_weight,
    post_gain,
    post_bias,
    merge_gain,
):
    chip_index = lax.axis_index("seq")
    core_index = lax.axis_index("enc")
    shards = lax.axis_size("seq")
    own_patches = PATCH_GROUP // lax.axis_size("enc")
    lengths = image_tokens[0]
    offsets = image_offset[0]
    owners = image_owner[0]
    live_slot, source, token_index, shard_row = slot_source(lengths, offsets, owners, chip_index)
    own_rows = lm_grad[0]
    global_row = source * ROWS_DEV + shard_row
    portion = lax.all_gather(own_rows, "seq", axis=1, tiled=True)
    row_count = portion.shape[1]
    inside_piece = live_slot & (global_row >= 0) & (global_row < row_count)
    taken = jnp.take(portion, jnp.clip(global_row, 0, row_count - 1), axis=1)
    incoming = jnp.where(inside_piece[None, :, None], taken, jnp.zeros_like(taken))
    res_grad, merge_grad, post_grad, shift_grad = head_back(
        incoming, layer_output[0], merge_gain, post_gain, post_bias
    )
    res_wire = res_grad.astype(jnp.bfloat16)
    all_res = lax.all_gather(res_wire, "enc", axis=0, tiled=True)
    input_rows = mlp_input[0]
    normed = (layer_norm(input_rows.astype(jnp.float32)) * pre_gain + pre_bias).astype(jnp.bfloat16)
    pre_act = (
        jnp.dot(normed.reshape(-1, D), fc1_weight, preferred_element_type=jnp.float32) + fc1_bias
    )
    down_back = lax.dot_general(
        all_res.reshape(-1, D),
        fc2_weight,
        (((1,), (1,)), ((), ())),
        preferred_element_type=jnp.float32,
    )
    hidden_grad = down_back * gelu_slope(pre_act)
    fc1_part = jnp.sum(hidden_grad, axis=0)
    hidden_units = fc1_bias.shape[0]
    hidden_wire = hidden_grad.astype(jnp.bfloat16).reshape(PATCH_GROUP, CAP_TOK, hidden_units)
    portion = hidden_wire
    product = lax.dot_general(
        portion.reshape(-1, hidden_units),
        fc1_weight,
        (((1,), (1,)), ((), ())),
        preferred_element_type=jnp.float32,
    )
    summed = lax.psum(product.reshape(PATCH_GROUP, CAP_TOK, D), "enc")
    upstream = lax.dynamic_slice_in_dim(summed, core_index * own_patches, own_patches, 0)
    own_input = lax.dynamic_slice_in_dim(input_rows, core_index * own_patches, own_patches, 0)
    input_grad, pre_scale_grad, pre_shift_grad = pre_back(own_input, pre_gain, pre_bias, upstream)
    act_grad = (res_grad + input_grad).astype(jnp.bfloat16)[None]
    fc2_part = jnp.sum(res_grad, axis=(0, 1))
    norm_part = jnp.stack(
        [merge_grad, post_grad, shift_grad, fc2_part, pre_scale_grad, pre_shift_grad]
    )
    fc1_full = lax.dynamic_update_slice_in_dim(
        jnp.zeros((FF,), jnp.float32), fc1_part, core_index * hidden_units, 0
    )
    norm_sum, fc1_sum = lax.psum((norm_part, fc1_full), ("seq", "dp", "enc"))
    grad_scale = 1.0 / math.sqrt(PATCH_GROUP * ROWS_DEV * shards * lax.axis_size("dp"))
    return (act_grad, norm_sum * grad_scale, fc1_sum * grad_scale)


def solution(mesh):
    in_specs = (
        P("dp", "enc", "seq", None),
        P("dp", None, None),
        P("dp", None, None),
        P("dp", None, None),
        P("dp", None, "seq", None),
        P("dp", "enc", "seq", None),
        P(),
        P(),
        P(None, "enc"),
        P("enc"),
        P("enc", None),
        P(),
        P(),
        P(),
    )
    out_specs = (P("dp", "enc", "seq", None), P(), P())
    return jax.shard_map(body, mesh=mesh, in_specs=in_specs, out_specs=out_specs, check_vma=False)
```

profile of v0, /device:TPU:0, one launch (start us, length us, event | category | flops | bytes accessed | tf_op | source)
XLA Modules:
  0.0 126.4 jit_solution(4036860565229651967)
XLA Ops:
  7.2 0.0 all-reduce.3.cloned.1.call-start
  7.2 0.9 select_reduce_fusion.2
  8.1 0.2 reduce-window.7
  8.3 0.1 fusion.43
  8.4 0.1 select_reduce_fusion.3
  8.5 1.3 %convert_reduce_fusion.2 = f32[4,60]{0,1:T(8,128)S(1)} fusion(bf16[1,4,60,1152]{3,1,2,0:T(4,128)(2,1)} %param.18), kind=kLoop, calls=%fused_computation.44 | loop fusion | flops 552720 | bytes 553920 | tf_op jit(solution)/shard_map/reduce_sum | solution.py:21
  9.9 1.6 %fusion.6 = f32[4,60]{0,1:T(8,128)S(1)} fusion(bf16[1,4,60,1152]{3,1,2,0:T(4,128)(2,1)} %param.18, f32[4,60]{0,1:T(8,128)S(1)} %broadcast_multiply_fusion.2), kind=kLoop, calls=%fused_computation.12 | loop fusion | flops 1105680 | bytes 554880 | tf_op jit(solution)/shard_map/reduce_sum | solution.py:23
  11.5 0.1 copy.81
  11.6 1.1 copy.66
  12.7 0.0 copy-start.5
  12.7 0.2 copy.52
  12.9 13.7 %all-gather = bf16[1,2,192,1152]{3,1,0,2:T(2,128)(2,1)S(1)} all-gather(bf16[1,2,48,1152]{3,1,0,2:T(2,128)(2,1)S(1)} %copy.52), channel_id=2, replica_groups=mesh['seq'=4,'dp'=4,'enc'=2] {'seq'}, dimensions={2}, use_global_device_ids=true | all-gather | bytes 1105920 | tf_op jit(solution)/shard_map/all_gather | solution.py:102
  26.6 0.3 convert_reduce_fusion.1
  26.9 0.5 fusion.14
  27.4 0.1 copy.55
  27.5 0.1 copy.56
  27.6 0.0 copy-done.3
  27.6 0.0 copy-done.4
  27.6 0.7 multiply_reduce_fusion.1
  28.3 0.1 copy.57
  28.4 0.1 copy.58
  28.6 1.2 gather_fusion
  29.7 1.7 %fusion.27 = (f32[1152]{0:T(1024)S(1)}, f32[2,60]{0,1:T(8,128)S(1)}, bf16[60,2,1152]{2,1,0:T(2,128)(2,1)S(1)}) fusion(f32[2,60]{0,1:T(8,128)S(1)} %copy.58, f32[1152]{0:T(1024)S(1)} %copy-done.4, f32[1152]{0:T(1024)S(1)} %copy-done.3, f32[2,60]{0,1:T(8,128)S(1)} %copy.56, f32[2,60]{0,1:T(8,128)S(1)} %broadcast_multiply_fusion.3, ...), kind=kLoop, calls=%fused_computation.43 | loop fusion | flops 1934088 | bytes 849912 | tf_op jit(solution)/shard_map/transpose(jvp())/reduce_sum | solution.py:41
  31.5 0.1 copy.59
  31.6 0.1 copy.60
  31.7 1.9 %multiply_reduce_fusion = (f32[1152]{0:T(1024)S(1)}, f32[2,60]{0,1:T(8,128)S(1)}, f32[1152]{0:T(1024)S(1)}, f32[2,60,1152]{2,0,1:T(2,128)S(1)}) fusion(bf16[1,2,60,1152]{3,1,2,0:T(2,128)(2,1)S(1)} %copy-done.1, f32[2,60]{0,1:T(8,128)S(1)} %copy.56, f32[2,60]{0,1:T(8,128)S(1)} %broadcast_multiply_fusion.3, f32[1152]{0:T(1024)S(1)} %copy-done.3, ...), kind=kLoop, calls=%fused_computation.45 | loop fusion | flops 2347656 | bytes 1131360 | tf_op jit(solution)/shard_map/transpose(jvp())/reduce_sum | solution.py:41
  33.6 0.1 copy.61
  33.7 0.1 copy.62
  33.8 0.8 fusion.42
  34.7 0.4 add_reduce_fusion
  35.1 0.0 copy-start.6
  35.1 0.0 copy-start.7
  35.1 0.0 copy-start.8
  35.1 2.5 %all_gather.7 = bf16[4,60,1152]{2,1,0:T(8,128)(2,1)S(1)} all-gather(bf16[2,60,1152]{2,1,0:T(8,128)(2,1)S(1)} %copy.65), channel_id=1, replica_groups=mesh['seq'=4,'dp'=4,'enc'=2] {'enc'}, dimensions={0}, use_global_device_ids=true | all-gather | bytes 829440 | tf_op jit(solution)/shard_map/all_gather | solution.py:111
  37.7 0.1 reshape.238
  37.8 0.1 copy.82
  37.9 0.1 rsqrt.44
  38.0 0.1 div.65
  38.0 0.1 reshape.240
  38.2 0.0 slice-start
  38.2 4.4 %convolution_add_fusion = f32[240,2152]{1,0:T(8,128)S(1)} fusion(bf16[1152,2152]{0,1:T(8,128)(2,1)} %param.22, f32[2152]{0:T(1024)S(1)} %copy-done.7, f32[240,1152]{1,0:T(8,128)S(1)} %reshape.240, f32[1152]{0:T(1024)S(1)} %copy-done.8, f32[1152]{0:T(1024)S(1)} %copy-done.6, f32[240]{0:T(256)S(1)} %rsqrt.44, f32[240]{0:T(256)S(1)} %div.65), kind=kOutput, calls=%fused_computation.2 | convolution fusion | flops 1191868800 | bytes 8149792 | tf_op jit(solution)/shard_map/dot_general | solution.py:115
  42.6 0.0 slice-start.1
  42.6 4.7 %fusion.45 = (f32[2152]{0:T(1024)S(1)}, bf16[240,2152]{1,0:T(8,128)(2,1)S(1)}) fusion(f32[240,2152]{1,0:T(8,128)S(1)} %convolution_add_fusion, bf16[240,1152]{1,0:T(8,128)(2,1)S(1)} %reshape.238, bf16[2152,1152]{1,0:T(8,128)(2,1)} %param.24), kind=kOutput, calls=%fused_computation.101 | convolution fusion | flops 1200297344 | bytes 8618656 | tf_op jit(solution)/shard_map/dot_general | solution.py:117
  47.3 0.0 slice-done
  47.4 1.6 %fusion.7 = f32[240,1152]{1,0:T(8,128)S(1)} fusion(bf16[1152,2152]{0,1:T(8,128)(2,1)S(1)} %bitcast.108, bf16[240,2152]{1,0:T(8,128)(2,1)S(1)} %get-tuple-element.31), kind=kOutput, calls=%fused_computation.14 | convolution fusion | flops 1189969920 | bytes 7097088 | tf_op jit(solution)/shard_map/dot_general | solution.py:128
  49.0 0.1 reshape.239
  49.1 0.0 copy-start
  49.1 1.8 %copy.70 = f32[4,60,1152]{2,0,1:T(4,128)} copy(f32[4,60,1152]{2,1,0:T(8,128)S(1)} %reshape.239) | data formatting | bytes 2211840 | tf_op jit(solution)/shard_map/reshape | solution.py:134
  50.9 0.0 all-reduce.3.cloned.1.call-update
  50.9 0.4 convert_reduce_fusion
  51.4 0.6 fusion.21
  52.0 0.1 copy.73
  52.0 0.1 copy.74
  52.2 0.3 dynamic_update_slice.3
  52.6 18.3 %all-reduce.3.cloned.1.call-done = f32[4,60,1152]{2,0,1:T(4,128)} async-done(((f32[4,60,1152]{2,0,1:T(4,128)}), f32[4,60,1152]{2,0,1:T(4,128)}) %all-reduce.3.cloned.1.call-update) | async-done | bytes 1105936 | tf_op jit(solution)/shard_map/psum | solution.py:134
  70.9 2.5 %fusion.32 = (f32[1152]{0:T(1024)S(1)}, f32[2,60]{0,1:T(8,128)S(1)}, f32[1152]{0:T(1024)S(1)}) fusion(f32[2,60]{0,1:T(8,128)S(1)} %copy.74, f32[2,60]{0,1:T(8,128)S(1)} %broadcast_multiply_fusion.1, f32[4,60,1152]{2,0,1:T(4,128)} %all-reduce.3.cloned.1.call-done, s32[]{:T(128)S(6)} %select_n.59, bf16[1,4,60,1152]{3,1,2,0:T(4,128)(2,1)S(1)} %copy-done, ...), kind=kLoop, calls=%fused_computation.53 | loop fusion | flops 1241736 | bytes 844708 | tf_op jit(solution)/shard_map/transpose(jvp())/reduce_sum | solution.py:52
  73.4 0.1 stack.27
  73.5 41.2 %all-reduce = (f32[6,1152]{1,0:T(8,128)S(1)}, f32[4304]{0:T(1024)S(1)}) all-reduce(f32[6,1152]{1,0:T(8,128)S(1)} %stack.27, f32[4304]{0:T(1024)S(1)} %dynamic_update_slice.3), channel_id=1, replica_groups=mesh['seq'=4,'dp'=4,'enc'=2] {'seq','dp','enc'}, use_global_device_ids=true, to_apply=%region_26.27 | all-reduce | flops 11216 | bytes 89728 | tf_op jit(solution)/shard_map/psum | solution.py:146
  114.7 0.6 broadcast_multiply_fusion
  115.3 0.6 broadcast_multiply_fusion.4
  115.9 0.1 copy.75
  116.0 0.1 copy.76
  116.1 2.3 %fusion.41 = (f32[2,60]{0,1:T(8,128)S(1)}, f32[2,60,1152]{2,0,1:T(2,128)S(1)}) fusion(f32[2,60]{0,1:T(8,128)S(1)} %copy.76, f32[2,60]{0,1:T(8,128)S(1)} %broadcast_multiply_fusion.1, bf16[1,4,60,1152]{3,1,2,0:T(4,128)(2,1)S(1)} %copy-done, s32[]{:T(128)S(6)} %select_n.59, f32[2,60]{0,1:T(8,128)S(1)} %copy.74, f32[1152]{0:T(1024)S(1)} %copy-done.6, ...), kind=kLoop, calls=%fused_computation.98 | loop fusion | flops 1105800 | bytes 1388932 | tf_op jit(solution)/shard_map/transpose(jvp())/reduce_sum | solution.py:22
  118.5 1.1 fusion.33
  (38 shorter events, 0.2 us)
Async XLA Ops:
  7.2 5.6 %copy-start.2 = (bf16[1,2,48,1152]{3,2,1,0:T(8,128)(2,1)S(1)}, bf16[1,2,48,1152]{3,2,1,0:T(8,128)(2,1)}, u32[]{:S(2)}) copy-start(bf16[1,2,48,1152]{3,2,1,0:T(8,128)(2,1)} %param.14) | copy-start | bytes 663556
  7.2 63.7 %all-reduce.3.cloned.1.call-start = ((), (), s32[]{:S(2)}) async-start(), calls=%async_computation | async-start | bytes 2211840 | tf_op jit(solution)/shard_map/psum | solution.py:134
  9.9 16.7 %copy-start.1 = (bf16[1,2,60,1152]{3,1,2,0:T(2,128)(2,1)S(1)}, bf16[1,2,60,1152]{3,1,2,0:T(2,128)(2,1)}, u32[]{:S(2)}) copy-start(bf16[1,2,60,1152]{3,1,2,0:T(2,128)(2,1)} %param.19) | copy-start | bytes 829444
  11.5 16.1 %copy-start.3 = (f32[1152]{0:T(1024)S(1)}, f32[1152]{0:T(1024)}, u32[]{:S(2)}) copy-start(f32[1152]{0:T(1024)} %param.25) | copy-start | bytes 13828
  11.5 16.1 %copy-start.4 = (f32[1152]{0:T(1024)S(1)}, f32[1152]{0:T(1024)}, u32[]{:S(2)}) copy-start(f32[1152]{0:T(1024)} %param.26) | copy-start | bytes 13828
  12.7 17.0 %copy-start.5 = (f32[1152]{0:T(1024)S(1)}, f32[1152]{0:T(1024)}, u32[]{:S(2)}) copy-start(f32[1152]{0:T(1024)} %param.27) | copy-start | bytes 13828
  35.1 3.1 %copy-start.6 = (f32[1152]{0:T(1024)S(1)}, f32[1152]{0:T(1024)}, u32[]{:S(2)}) copy-start(f32[1152]{0:T(1024)} %param.20) | copy-start | bytes 13828
  35.1 3.1 %copy-start.7 = (f32[2152]{0:T(1024)S(1)}, f32[2152]{0:T(1024)}, u32[]{:S(2)}) copy-start(f32[2152]{0:T(1024)} %param.23) | copy-start | bytes 25828
  35.1 3.1 %copy-start.8 = (f32[1152]{0:T(1024)S(1)}, f32[1152]{0:T(1024)}, u32[]{:S(2)}) copy-start(f32[1152]{0:T(1024)} %param.21) | copy-start | bytes 13828
  38.2 9.1 %slice-start = ((s8[4958208]{0:T(1024)(128)(4,1)}), s8[4194304]{0:T(1024)(128)(4,1)S(1)}, s32[]{:S(2)}) async-start(s8[4958208]{0:T(1024)(128)(4,1)} %bitcast.107), calls=%async_computation.1 | async-start | bytes 8388608
  42.6 4.7 %slice-start.1 = ((s8[4958208]{0:T(1024)(128)(4,1)}), s8[763904]{0:T(1024)(128)(4,1)S(1)}, s32[]{:S(2)}) async-start(s8[4958208]{0:T(1024)(128)(4,1)} %bitcast.107), calls=%async_computation.2 | async-start | bytes 1527808
  49.1 1.8 %copy-start = (bf16[1,4,60,1152]{3,1,2,0:T(4,128)(2,1)S(1)}, bf16[1,4,60,1152]{3,1,2,0:T(4,128)(2,1)}, u32[]{:S(2)}) copy-start(bf16[1,4,60,1152]{3,1,2,0:T(4,128)(2,1)} %param.18) | copy-start | bytes 1658884
Sparse Core Ops, SparseCore 0:
  51.0 19.8 all-reduce.2
where the time goes:
time: 127 us; the launch traced here: 126 us
  blocking collectives  57.4 us (45%)
  other arithmetic  19 us (15%)
  waiting for transfers between devices  18.3 us (14%)
  between operations  14.4 us (11%)
  matrix products  10.7 us (8%)
  local copies, waits for them, and re-layouts  6.55 us (5%)
    psum x1, blocking collectives, body(): norm_sum, fc1_sum = lax.psum((norm_part, fc1_full), ('seq', 'dp', 'enc'))  41.2 us
    psum x1, waiting for transfers between devices, body(): summed = lax.psum(product.reshape(PATCH_GROUP, CAP_TOK, D), 'enc')  18.3 us
    all_gather x1, blocking collectives, body(): portion = lax.all_gather(own_rows, 'seq', axis=1, tiled=True)  13.7 us
    dot_general x1, matrix products, body(): lax.dot_general(all_res.reshape(-1, D), fc2_weight, (((1,), (1,)), ((), (...  4.7 us
    dot_general x1, matrix products, body(): jnp.dot(normed.reshape(-1, D), fc1_weight, preferred_element_type=jnp.flo...  4.4 us
    reduce_sum x2, other arithmetic, layer_norm(): centred = values - row_mean  3.14 us
    reduce_sum x3, other arithmetic, layer_norm(): jnp.mean(centred * centred, axis=-1, keepdims=True) + EPSILON  2.67 us
    all_gather x1, blocking collectives, body(): all_res = lax.all_gather(res_wire, 'enc', axis=0, tiled=True)  2.54 us
  transfers between devices with their start and end apart: 1, of which 1 were waited for; matrix products, arithmetic and copies ran while one was open for 1% of the time, Pallas kernels for 0%

commit v1 on v0

v1 whole, which is shorter than its diff:
```python
import math

import jax
import jax.numpy as jnp
from jax import lax
from jax.experimental import pallas as pl
from jax.experimental.pallas import tpu as pltpu
from jax.sharding import PartitionSpec as P

MOST_LEN = 15
WINDOW = 16
SUBLANES = 8
EPSILON = 1e-06
SLOPE_K = math.sqrt(2.0 / math.pi)
CUBIC = 0.044715
F32 = jnp.float32
BF16 = jnp.bfloat16
MESH_ID = pl.DeviceIdType.MESH


def gelu_slope(pre_act):
    inner_arg = SLOPE_K * (pre_act + CUBIC * pre_act * pre_act * pre_act)
    tangent = jnp.tanh(inner_arg)
    return 0.5 * (1.0 + tangent) + 0.5 * pre_act * (1.0 - tangent * tangent) * SLOPE_K * (
        1.0 + 3.0 * CUBIC * pre_act * pre_act
    )


def row_mean(values):
    return jnp.mean(values, axis=-1, keepdims=True)


def norm_parts(values):
    centred = values - row_mean(values)
    scale = lax.rsqrt(row_mean(centred * centred) + EPSILON)
    return centred * scale, scale


def norm_pull(normal, scale, cotangent):
    return scale * (cotangent - row_mean(cotangent) - normal * row_mean(cotangent * normal))


def greet(peers):
    barrier = pltpu.get_barrier_semaphore()
    for peer in peers:
        pl.semaphore_signal(barrier, inc=1, device_id=peer, device_id_type=MESH_ID)
    return lambda: pl.semaphore_wait(barrier, len(peers))


def others(axis, count):
    me = lax.axis_index(axis)
    return [{axis: lax.rem(me + step, count)} for step in range(1, count)]


def remote(src, dst, send_sem, recv_sem, peer):
    copy = pltpu.make_async_remote_copy(
        src_ref=src,
        dst_ref=dst,
        send_sem=send_sem,
        recv_sem=recv_sem,
        device_id=peer,
        device_id_type=MESH_ID,
    )
    copy.start()
    return copy


def head_kernel(
    shards,
    pack_ref,
    unpack_ref,
    grad_ref,
    layer_ref,
    input_ref,
    pre_gain_ref,
    pre_bias_ref,
    post_gain_ref,
    post_bias_ref,
    merge_ref,
    all_ref,
    res_ref,
    normed_ref,
    sums_ref,
    send_buf,
    recv_buf,
    swap_out,
    swap_in,
    seq_send,
    seq_recv,
    enc_send,
    enc_recv,
):
    me = lax.axis_index("seq")
    core = lax.axis_index("enc")
    partner = {"enc": 1 - core}
    own, rows_dev, width = grad_ref.shape
    slots = layer_ref.shape[1]
    peers = others("seq", shards)
    settle = greet([partner] + peers)
    for patch in range(own):
        packed = jnp.dot(pack_ref[...], grad_ref[patch], preferred_element_type=F32)
        send_buf[:, patch] = packed.astype(BF16).reshape(shards, WINDOW, width)
    settle()
    copies = []
    for step, peer in enumerate(peers):
        copies.append(
            remote(
                send_buf.at[peer["seq"]],
                recv_buf.at[me],
                seq_send.at[step],
                seq_recv.at[step],
                peer,
            )
        )
    recv_buf[me] = send_buf[me]
    pre_gain = pre_gain_ref[...]
    pre_bias = pre_bias_ref[...]
    normed_ref[...] = jnp.zeros_like(normed_ref)
    for patch in range(input_ref.shape[0]):
        normal, _ = norm_parts(input_ref[patch].astype(F32))
        normed_ref[patch, 0:slots, :] = (normal * pre_gain + pre_bias).astype(BF16)
    post_gain = post_gain_ref[...]
    post_bias = post_bias_ref[...]
    merge_gain = merge_ref[...]
    swap_out[...] = jnp.zeros_like(swap_out)
    for copy in copies:
        copy.wait()
    swaps = []
    totals = None
    for patch in range(own):
        landed = recv_buf[:, patch].reshape(shards * WINDOW, width)
        incoming = jnp.dot(unpack_ref[...], landed, preferred_element_type=F32)
        normal, scale = norm_parts(layer_ref[patch].astype(F32))
        affine = normal * post_gain + post_bias
        rms = lax.rsqrt(row_mean(affine * affine) + EPSILON)
        unit = affine * rms
        unit_grad = incoming * merge_gain
        affine_grad = rms * (unit_grad - unit * row_mean(unit_grad * unit))
        res = norm_pull(normal, scale, affine_grad * post_gain)
        res_ref[patch] = res
        swap_out[patch, 0:slots, :] = res.astype(BF16)
        parts = [
            jnp.sum(term, axis=0, keepdims=True)
            for term in (incoming * unit, affine_grad * normal, affine_grad, res)
        ]
        totals = parts if totals is None else [a + b for a, b in zip(totals, parts)]
        swaps.append(
            remote(
                swap_out.at[patch],
                swap_in.at[patch],
                enc_send.at[patch],
                enc_recv.at[patch],
                partner,
            )
        )
        all_ref[core * own + patch] = swap_out[patch]
    sums_ref[...] = jnp.zeros_like(sums_ref)
    for index, total in enumerate(totals):
        sums_ref[index : index + 1, :] = total
    for patch in range(own):
        swaps[patch].wait()
        all_ref[(1 - core) * own + patch] = swap_in[patch]


def tail_kernel(
    shards,
    replicas,
    grad_scale,
    product_ref,
    input_ref,
    pre_gain_ref,
    res_ref,
    sums_ref,
    units_ref,
    act_ref,
    total_ref,
    swap_in,
    halves,
    half_in,
    seq_buf,
    dp_buf,
    last_buf,
    enc_send,
    enc_recv,
    seq_send,
    seq_recv,
    dp_send,
    dp_recv,
):
    me = lax.axis_index("seq")
    replica = lax.axis_index("dp")
    core = lax.axis_index("enc")
    other = 1 - core
    partner = {"enc": other}
    own = act_ref.shape[0]
    slots = act_ref.shape[1]
    seq_peers = others("seq", shards)
    dp_peers = others("dp", replicas)
    settle = greet([partner] + seq_peers + dp_peers)
    halves[...] = jnp.zeros_like(halves)
    unit_rows = units_ref.shape[0]
    halves[0, 0:1, :] = sums_ref[0:1, :]
    halves[0, 1:2, :] = sums_ref[1:2, :]
    halves[0, 2:3, :] = sums_ref[2:3, :]
    halves[1, 0:1, :] = sums_ref[3:4, :]
    for index in range(unit_rows):
        halves[core, 3 + index : 4 + index, :] = units_ref[index : index + 1, :]
    settle()
    swaps = [
        remote(
            product_ref.at[other * own + patch],
            swap_in.at[patch],
            enc_send.at[patch],
            enc_recv.at[patch],
            partner,
        )
        for patch in range(own)
    ]
    pre_gain = pre_gain_ref[...]
    gain_grad = None
    for patch in range(own):
        normal, scale = norm_parts(input_ref[core * own + patch].astype(F32))
        swaps[patch].wait()
        upstream = product_ref[core * own + patch, 0:slots, :] + swap_in[patch, 0:slots, :]
        parts = [
            jnp.sum(upstream * normal, axis=0, keepdims=True),
            jnp.sum(upstream, axis=0, keepdims=True),
        ]
        gain_grad = parts if gain_grad is None else [a + b for a, b in zip(gain_grad, parts)]
        act = res_ref[patch] + norm_pull(normal, scale, upstream * pre_gain)
        act_ref[patch] = act.astype(BF16)
    halves[1, 1:2, :] = gain_grad[0]
    halves[1, 2:3, :] = gain_grad[1]
    remote(halves.at[other], half_in, enc_send.at[own], enc_recv.at[own], partner).wait()
    seq_buf[me] = halves[core] + half_in[...]
    copies = [
        remote(seq_buf.at[me], seq_buf.at[me], seq_send.at[step], seq_recv.at[step], peer)
        for step, peer in enumerate(seq_peers)
    ]
    for copy in copies:
        copy.wait()
    total = seq_buf[0]
    for index in range(1, shards):
        total = total + seq_buf[index]
    dp_buf[replica] = total
    copies = [
        remote(dp_buf.at[replica], dp_buf.at[replica], dp_send.at[step], dp_recv.at[step], peer)
        for step, peer in enumerate(dp_peers)
    ]
    for copy in copies:
        copy.wait()
    total = dp_buf[0]
    for index in range(1, replicas):
        total = total + dp_buf[index]
    last_buf[core] = total * grad_scale
    remote(
        last_buf.at[core], last_buf.at[core], enc_send.at[own + 1], enc_recv.at[own + 1], partner
    ).wait()
    total_ref[...] = last_buf[...]


def round_up(value, step):
    return (value + step - 1) // step * step


def body(
    lm_grad,
    image_tokens,
    image_offset,
    image_owner,
    mlp_input,
    layer_output,
    pre_gain,
    pre_bias,
    fc1_weight,
    fc1_bias,
    fc2_weight,
    post_gain,
    post_bias,
    merge_gain,
):
    me = lax.axis_index("seq")
    shards = lax.axis_size("seq")
    replicas = lax.axis_size("dp")
    cores = lax.axis_size("enc")
    grad_rows = lm_grad[0]
    input_rows = mlp_input[0]
    layer_rows = layer_output[0]
    own, rows_dev, width = grad_rows.shape
    group, slots, _ = input_rows.shape
    padded = round_up(slots, WINDOW)
    lengths, offsets, owners = image_tokens[0], image_offset[0], image_owner[0]

    chips = jnp.arange(shards, dtype=jnp.int32)
    steps = jnp.arange(WINDOW, dtype=jnp.int32)
    my_images = lax.dynamic_slice_in_dim(jnp.stack([lengths, offsets, owners]), me, 1, 1)[:, 0]
    to_chip = my_images[2][None, :] == chips[:, None]
    sent_len = jnp.sum(jnp.where(to_chip, my_images[0][None, :], 0), axis=1)
    sent_off = jnp.sum(jnp.where(to_chip, my_images[1][None, :], 0), axis=1)
    source_row = jnp.where(
        steps[None, :] < sent_len[:, None], sent_off[:, None] + steps[None, :], -1
    ).reshape(-1)
    pack = (source_row[:, None] == jnp.arange(rows_dev, dtype=jnp.int32)[None, :]).astype(BF16)
    mine_len = jnp.sum(jnp.where(owners == me, lengths, 0), axis=1)
    first = jnp.sum(jnp.where(chips[None, :] < chips[:, None], mine_len[None, :], 0), axis=1)
    target_slot = jnp.where(
        steps[None, :] < mine_len[:, None], first[:, None] + steps[None, :], -1
    ).reshape(-1)
    unpack = (jnp.arange(slots, dtype=jnp.int32)[:, None] == target_slot[None, :]).astype(BF16)

    vmem = pl.BlockSpec(memory_space=pltpu.VMEM)
    dma = pltpu.SemaphoreType.DMA
    gain_row = pre_gain.reshape(1, width)

    def head_call(*refs):
        head_kernel(shards, *refs)

    all_res, res_grad, normed, sums = pl.pallas_call(
        head_call,
        out_shape=(
            jax.ShapeDtypeStruct((group, padded, width), BF16),
            jax.ShapeDtypeStruct((own, slots, width), F32),
            jax.ShapeDtypeStruct((group, padded, width), BF16),
            jax.ShapeDtypeStruct((SUBLANES, width), F32),
        ),
        in_specs=[vmem] * 10,
        out_specs=(vmem,) * 4,
        scratch_shapes=[
            pltpu.VMEM((shards, own, WINDOW, width), BF16),
            pltpu.VMEM((shards, own, WINDOW, width), BF16),
            pltpu.VMEM((own, padded, width), BF16),
            pltpu.VMEM((own, padded, width), BF16),
            dma((shards - 1,)),
            dma((shards - 1,)),
            dma((own,)),
            dma((own,)),
        ],
        compiler_params=pltpu.CompilerParams(collective_id=0, has_side_effects=True),
        name="head",
    )(
        pack,
        unpack,
        grad_rows,
        layer_rows,
        input_rows,
        gain_row,
        pre_bias.reshape(1, width),
        post_gain.reshape(1, width),
        post_bias.reshape(1, width),
        merge_gain.reshape(1, width),
    )

    pre_act = (
        jnp.dot(normed.reshape(-1, width), fc1_weight, preferred_element_type=F32) + fc1_bias
    )
    down_back = lax.dot_general(
        all_res.reshape(-1, width),
        fc2_weight,
        (((1,), (1,)), ((), ())),
        preferred_element_type=F32,
    )
    hidden_grad = down_back * gelu_slope(pre_act)
    fc1_part = jnp.sum(hidden_grad, axis=0)
    hidden_units = fc1_bias.shape[0]
    product = lax.dot_general(
        hidden_grad.astype(BF16),
        fc1_weight,
        (((1,), (1,)), ((), ())),
        preferred_element_type=F32,
    ).reshape(group, padded, width)
    unit_rows = round_up(hidden_units, width) // width
    units = jnp.pad(fc1_part, (0, unit_rows * width - hidden_units)).reshape(unit_rows, width)

    grad_scale = 1.0 / math.sqrt(group * rows_dev * shards * replicas)
    sum_rows = round_up(3 + unit_rows, SUBLANES)

    def tail_call(*refs):
        tail_kernel(shards, replicas, grad_scale, *refs)

    act_grad, totals = pl.pallas_call(
        tail_call,
        out_shape=(
            jax.ShapeDtypeStruct((own, slots, width), BF16),
            jax.ShapeDtypeStruct((cores, sum_rows, width), F32),
        ),
        in_specs=[vmem] * 6,
        out_specs=(vmem,) * 2,
        scratch_shapes=[
            pltpu.VMEM((own, padded, width), F32),
            pltpu.VMEM((cores, sum_rows, width), F32),
            pltpu.VMEM((sum_rows, width), F32),
            pltpu.VMEM((shards, sum_rows, width), F32),
            pltpu.VMEM((replicas, sum_rows, width), F32),
            pltpu.VMEM((cores, sum_rows, width), F32),
            dma((own + 2,)),
            dma((own + 2,)),
            dma((shards - 1,)),
            dma((shards - 1,)),
            dma((replicas - 1,)),
            dma((replicas - 1,)),
        ],
        compiler_params=pltpu.CompilerParams(collective_id=1, has_side_effects=True),
        name="tail",
    )(product, input_rows, gain_row, res_grad, sums, units)
    norm_grads = totals[:, :3].reshape(-1, width)
    fc1_grad = totals[:, 3 : 3 + unit_rows].reshape(cores, -1)[:, :hidden_units].reshape(-1)
    return (act_grad[None], norm_grads, fc1_grad)


def solution(mesh):
    in_specs = (
        P("dp", "enc", "seq", None),
        P("dp", None, None),
        P("dp", None, None),
        P("dp", None, None),
        P("dp", None, "seq", None),
        P("dp", "enc", "seq", None),
        P(),
        P(),
        P(None, "enc"),
        P("enc"),
        P("enc", None),
        P(),
        P(),
        P(),
    )
    out_specs = (P("dp", "enc", "seq", None), P(), P())
    return jax.shard_map(body, mesh=mesh, in_specs=in_specs, out_specs=out_specs, check_vma=False)
```

time: 127 us -> 64 us (0.50)
  blocking collectives: 57.4 us -> 0 us
  Pallas kernels: 0 us -> 31 us
  waiting for transfers between devices: 18.3 us -> 0 us
  other arithmetic: 19 us -> 3.25 us
  between operations: 14.4 us -> 0.75 us
  local copies, waits for them, and re-layouts: 6.55 us -> 16 us
  matrix products: 10.7 us -> 12.2 us
    psum x1 -> x0, blocking collectives: 41.2 us -> none  [body(): norm_sum, fc1_sum = lax.psum((norm_part, fc1_full), ('seq', 'dp', 'enc'))]
    pallas_call x0 -> x2, Pallas kernels: none -> 31 us  [the longest x1 18 us: body(): pl.pallas_call(tail_call, out_shape=(jax.ShapeDtypeStruct((own, slots, wi...]
    psum x1 -> x0, waiting for transfers between devices: 18.3 us -> none  [body(): summed = lax.psum(product.reshape(PATCH_GROUP, CAP_TOK, D), 'enc')]
    all_gather x2 -> x0, blocking collectives: 16.2 us -> none  [the longest x1 13.7 us: body(): portion = lax.all_gather(own_rows, 'seq', axis=1, tiled=True)]
    reduce_sum x15 -> x3, other arithmetic: 16.2 us -> 1.08 us  [the longest x1 0.82 us: body(): mine_len = jnp.sum(jnp.where(owners == me, lengths, 0), axis=1)]
    reshape x3 -> x8, local copies, waits for them, and re-layouts: 1.98 us -> 8.4 us  [the longest x1 1.3 us: body(): gain_row = pre_gain.reshape(1, width)]
    unnamed x25 -> x13, local copies, waits for them, and re-layouts: 0.4 us -> 6.54 us
    dot_general x3, matrix products: 10.7 us -> 12.2 us  [the longest x1 5.13 us: body(): lax.dot_general(hidden_grad.astype(BF16), fc1_weight, (((1,), (1,)), ((),...]
  transfers between devices with their start and end apart: 1 -> 0, of which waited for: 1 -> 0; matrix products, arithmetic and copies ran while one was open for 1% -> 0% of each run, Pallas kernels for 0% -> 0%
where the time goes in v1:
time: 64 us; the launch traced here: 63.3 us
  Pallas kernels  31 us (48%)
  local copies, waits for them, and re-layouts  16 us (25%)
  matrix products  12.2 us (19%)
  other arithmetic  3.25 us (5%)
  between operations  0.75 us (1%)
    pallas_call x1, Pallas kernels, body(): pl.pallas_call(tail_call, out_shape=(jax.ShapeDtypeStruct((own, slots, wi...  18 us
    pallas_call x1, Pallas kernels, body(): pl.pallas_call(head_call, out_shape=(jax.ShapeDtypeStruct((group, padded,...  13 us
    unnamed x13, local copies, waits for them, and re-layouts  6.54 us
    dot_general x1, matrix products, body(): lax.dot_general(hidden_grad.astype(BF16), fc1_weight, (((1,), (1,)), ((),...  5.13 us
    dot_general x1, matrix products, body(): jnp.dot(normed.reshape(-1, width), fc1_weight, preferred_element_type=F32)  4.38 us
    dot_general x1, matrix products, body(): lax.dot_general(all_res.reshape(-1, width), fc2_weight, (((1,), (1,)), ((...  2.72 us
    reshape x1, local copies, waits for them, and re-layouts, body(): gain_row = pre_gain.reshape(1, width)  1.3 us
    reshape x1, local copies, waits for them, and re-layouts, body(): merge_gain.reshape(1, width)  1.29 us

profile of v1, /device:TPU:0, one launch (start us, length us, event | category | flops | bytes accessed | tf_op | source)
XLA Modules:
  0.0 63.3 jit_solution(8608999036555279501)
XLA Ops:
  0.6 0.0 copy-start.1
  0.6 0.8 %select_reduce_fusion.1 = s32[4]{0:T(128)S(1)} fusion(s32[1,4,4]{2,1,0:T(4,128)} %param.15, s32[1,4,4]{2,1,0:T(4,128)} %param.17, s32[]{:T(128)S(6)} %axis_index.15), kind=kLoop, calls=%fused_computation.24 | loop fusion | flops 44 | bytes 148 | tf_op jit(solution)/shard_map/reduce_sum | solution.py:304
  1.5 0.1 select_reduce_fusion
  1.6 0.1 add_select_fusion
  1.7 0.1 select_n.47
  1.7 0.7 %fusion.10 = s32[3,1,4]{2,1,0:T(1,128)S(1)} fusion(s32[]{:T(128)S(6)} %select_n.39, s32[1,4,4]{2,1,0:T(4,128)} %param.15, s32[1,4,4]{2,1,0:T(4,128)} %param.16, s32[1,4,4]{2,1,0:T(4,128)} %param.17), kind=kLoop, calls=%fused_computation.32 | loop fusion | flops 24 | bytes 244 | tf_op jit(solution)/shard_map/stack | solution.py:296
  2.5 0.1 select_reduce_fusion.3
  2.6 0.1 add_select_fusion.1
  2.7 0.1 select_n.43
  2.8 1.3 %reshape.120.refs_5_.refs_2_ = f32[1,1152]{1,0:T(1,128)} reshape(f32[1152]{0:T(1024)} %param.20) | data formatting | bytes 9216 | tf_op jit(solution)/shard_map/reshape | solution.py:313
  4.1 1.3 %reshape.121.refs_6_ = f32[1,1152]{1,0:T(1,128)} reshape(f32[1152]{0:T(1024)} %param.21) | data formatting | bytes 9216 | tf_op jit(solution)/shard_map/reshape | solution.py:347
  5.4 1.3 %reshape.122.refs_7_ = f32[1,1152]{1,0:T(1,128)} reshape(f32[1152]{0:T(1024)} %param.25) | data formatting | bytes 9216 | tf_op jit(solution)/shard_map/reshape | solution.py:348
  6.7 1.3 %reshape.123.refs_8_ = f32[1,1152]{1,0:T(1,128)} reshape(f32[1152]{0:T(1024)} %param.26) | data formatting | bytes 9216 | tf_op jit(solution)/shard_map/reshape | solution.py:349
  8.0 1.3 %reshape.124.refs_9_ = f32[1,1152]{1,0:T(1,128)} reshape(f32[1152]{0:T(1024)} %param.27) | data formatting | bytes 9216 | tf_op jit(solution)/shard_map/reshape | solution.py:350
  9.2 0.7 %fusion.7.refs_0_ = bf16[64,48]{1,0:T(8,128)(2,1)} fusion(s32[64]{0:T(128)S(1)} %select_n.43), kind=kLoop, calls=%fused_computation.15 | loop fusion | flops 6144 | bytes 6400 | tf_op jit(solution)/shard_map/convert_element_type | solution.py:303
  9.9 0.6 fusion.8.refs_1_
  10.5 1.7 %copy.30 = bf16[1,2,60,1152]{3,2,1,0:T(8,128)(2,1)} copy(bf16[1,2,60,1152]{3,1,2,0:T(2,128)(2,1)} %param.19) | data formatting | bytes 552960 | tf_op args[5]
  12.2 2.0 %copy.29 = bf16[1,4,60,1152]{3,2,1,0:T(8,128)(2,1)} copy(bf16[1,4,60,1152]{3,1,2,0:T(4,128)(2,1)} %param.18) | data formatting | bytes 1105920 | tf_op args[4]
  14.2 0.0 slice-start
  14.2 13.0 %head.1 = (bf16[4,64,1152]{2,1,0:T(8,128)(2,1)}, f32[2,60,1152]{2,1,0:T(8,128)}, bf16[4,64,1152]{2,1,0:T(8,128)(2,1)}, f32[8,1152]{1,0:T(8,128)}) custom-call(bf16[64,48]{1,0:T(8,128)(2,1)} %fusion.7.refs_0_, bf16[60,64]{1,0:T(8,128)(2,1)} %fusion.8.refs_1_, bf16[2,48,1152]{2,1,0:T(8,128)(2,1)} %bitcast.31, bf16[2,60,1152]{2,1,0:T(8,128)(2,1)} %bitcast.29, ...), custom_call_target="tpu_custom_call" | custom-call | tf_op jit(solution)/shard_map/head/pallas_call | solution.py:318
  27.2 0.0 copy-done.1
  27.2 0.0 slice-start.1
  27.2 0.0 copy-start
  27.2 4.4 %convolution_add_fusion = f32[256,2152]{0,1:T(8,128)S(1)} fusion(bf16[256,1152]{1,0:T(8,128)(2,1)} %bitcast.36, bf16[1152,2152]{0,1:T(8,128)(2,1)} %param.22, f32[2152]{0:T(1024)S(1)} %copy-done.1), kind=kOutput, calls=%fused_computation.1 | convolution fusion | flops 1269852160 | bytes 7760288 | tf_op jit(solution)/shard_map/dot_general | solution.py:354
  31.6 0.0 slice-done
  31.6 0.0 slice-done.1
  31.6 0.0 copy-done
  31.7 2.7 %fusion.11 = (f32[2152]{0:T(1024)S(1)}, bf16[256,2152]{0,1:T(8,128)(2,1)S(1)}) fusion(f32[256,2152]{0,1:T(8,128)S(1)} %convolution_add_fusion, bf16[256,1152]{1,0:T(8,128)(2,1)S(1)} %bitcast.35, bf16[2152,1152]{1,0:T(8,128)(2,1)S(1)} %bitcast.34), kind=kOutput, calls=%fused_computation.36 | convolution fusion | flops 1280317312 | bytes 8862112 | tf_op jit(solution)/shard_map/dot_general | solution.py:356
  34.4 0.6 reshape.128.refs_5_
  35.0 5.1 %fusion.5 = f32[256,1152]{1,0:T(8,128)} fusion(bf16[1152,2152]{0,1:T(8,128)(2,1)} %param.22, bf16[256,2152]{0,1:T(8,128)(2,1)S(1)} %get-tuple-element.30), kind=kOutput, calls=%fused_computation.9 | convolution fusion | flops 1269301248 | bytes 7239680 | tf_op jit(solution)/shard_map/dot_general | solution.py:365
  40.1 18.0 %tail.1 = (bf16[2,60,1152]{2,1,0:T(8,128)(2,1)}, f32[2,8,1152]{2,1,0:T(8,128)}) custom-call(f32[4,64,1152]{2,1,0:T(8,128)} %bitcast.28, bf16[4,60,1152]{2,1,0:T(8,128)(2,1)} %bitcast.27, f32[1,1152]{1,0:T(1,128)} %reshape.120.refs_5_.refs_2_, f32[2,60,1152]{2,1,0:T(8,128)} %get-tuple-element.11.refs_3_, f32[8,1152]{1,0:T(8,128)} %get-tuple-element.12.refs_4_, ...), custom_call_target="tpu_custom_call" | custom-call | tf_op jit(solution)/shard_map/tail/pallas_call | solution.py:380
  58.2 2.0 %copy.25 = bf16[1,2,60,1152]{3,1,2,0:T(2,128)(2,1)} copy(bf16[1,2,60,1152]{3,2,1,0:T(8,128)(2,1)} %bitcast.30) | data formatting | bytes 552960
  60.1 0.9 %slice_bitcast_fusion = f32[1,2,2,1152]{3,2,1,0:T(2,128)S(1)} fusion(f32[2,8,1152]{2,1,0:T(8,128)} %get-tuple-element.14), kind=kLoop, calls=%fused_computation.17 | loop fusion | bytes 36864
  61.0 0.9 %slice.24 = f32[2,3,1152]{2,1,0:T(4,128)S(1)} slice(f32[2,8,1152]{2,1,0:T(8,128)} %get-tuple-element.14), slice={[0:2], [0:3], [0:1152]} | slice | bytes 55296 | tf_op jit(solution)/shard_map/slice | solution.py:405
  61.9 0.6 %reshape.129 = f32[6,1152]{1,0:T(8,128)} reshape(f32[2,3,1152]{2,1,0:T(4,128)S(1)} %slice.24) | data formatting | bytes 55296 | tf_op jit(solution)/shard_map/reshape | solution.py:405
  62.6 0.7 %reshape.131 = f32[4304]{0:T(1024)} reshape(f32[2,2152]{1,0:T(2,128)S(1)} %slice.30) | data formatting | bytes 34432 | tf_op jit(solution)/shard_map/reshape | solution.py:406
  (5 shorter events, 0.0 us)
Async XLA Ops:
  0.6 26.6 %copy-start.1 = (f32[2152]{0:T(1024)S(1)}, f32[2152]{0:T(1024)}, u32[]{:S(2)}) copy-start(f32[2152]{0:T(1024)} %param.23) | copy-start | bytes 25828
  14.2 17.4 %slice-start = ((s8[4958208]{0:T(1024)(128)(4,1)}), s8[763904]{0:T(1024)(128)(4,1)S(1)}, s32[]{:S(2)}) async-start(s8[4958208]{0:T(1024)(128)(4,1)} %bitcast.33), calls=%async_computation | async-start | bytes 1527808
  27.2 4.4 %slice-start.1 = ((s8[4958208]{0:T(1024)(128)(4,1)}), s8[4194304]{0:T(1024)(128)(4,1)S(1)}, s32[]{:S(2)}) async-start(s8[4958208]{0:T(1024)(128)(4,1)} %bitcast.33), calls=%async_computation.1 | async-start | bytes 8388608
  27.2 4.4 %copy-start = (bf16[4,64,1152]{2,1,0:T(8,128)(2,1)S(1)}, bf16[4,64,1152]{2,1,0:T(8,128)(2,1)}, u32[]{:S(2)}) copy-start(bf16[4,64,1152]{2,1,0:T(8,128)(2,1)} %get-tuple-element.9) | copy-start | bytes 1769476

commit v2 on v1

--- a/solution.py
+++ b/solution.py
@@ -10,6 +10,7 @@
 MOST_LEN = 15
 WINDOW = 16
 SUBLANES = 8
+HEAD_VMEM = 24 * 1024 * 1024
 EPSILON = 1e-06
 SLOPE_K = math.sqrt(2.0 / math.pi)
 CUBIC = 0.044715
@@ -67,8 +68,9 @@
 
 def head_kernel(
     shards,
-    pack_ref,
-    unpack_ref,
+    tokens_ref,
+    offsets_ref,
+    owners_ref,
     grad_ref,
     layer_ref,
     input_ref,
@@ -97,8 +99,18 @@
     slots = layer_ref.shape[1]
     peers = others("seq", shards)
     settle = greet([partner] + peers)
-    for patch in range(own):
-        packed = jnp.dot(pack_ref[...], grad_ref[patch], preferred_element_type=F32)
+    images = tokens_ref.shape[1]
+    places = shards * WINDOW
+    place = lax.broadcasted_iota(jnp.int32, (places, rows_dev), 0)
+    chip, step = place // WINDOW, place % WINDOW
+    source = jnp.full((places, rows_dev), -1, jnp.int32)
+    for image in range(images):
+        taken = (chip == owners_ref[me, image]) & (step < tokens_ref[me, image])
+        source = jnp.where(taken, offsets_ref[me, image] + step, source)
+    row = lax.broadcasted_iota(jnp.int32, (places, rows_dev), 1)
+    pack = jnp.where(row == source, 1.0, 0.0).astype(BF16)
+    for patch in range(own):
+        packed = jnp.dot(pack, grad_ref[patch], preferred_element_type=F32)
         send_buf[:, patch] = packed.astype(BF16).reshape(shards, WINDOW, width)
     settle()
     copies = []
@@ -113,23 +125,35 @@
             )
         )
     recv_buf[me] = send_buf[me]
-    pre_gain = pre_gain_ref[...]
-    pre_bias = pre_bias_ref[...]
+    pre_gain = pre_gain_ref[...].reshape(1, -1)
+    pre_bias = pre_bias_ref[...].reshape(1, -1)
     normed_ref[...] = jnp.zeros_like(normed_ref)
     for patch in range(input_ref.shape[0]):
         normal, _ = norm_parts(input_ref[patch].astype(F32))
         normed_ref[patch, 0:slots, :] = (normal * pre_gain + pre_bias).astype(BF16)
-    post_gain = post_gain_ref[...]
-    post_bias = post_bias_ref[...]
-    merge_gain = merge_ref[...]
+    post_gain = post_gain_ref[...].reshape(1, -1)
+    post_bias = post_bias_ref[...].reshape(1, -1)
+    merge_gain = merge_ref[...].reshape(1, -1)
     swap_out[...] = jnp.zeros_like(swap_out)
+    place = lax.broadcasted_iota(jnp.int32, (slots, places), 1)
+    chip, step = place // WINDOW, place % WINDOW
+    target = jnp.full((slots, places), -1, jnp.int32)
+    first = jnp.int32(0)
+    for shard in range(shards):
+        count = jnp.int32(0)
+        for image in range(images):
+            count += jnp.where(owners_ref[shard, image] == me, tokens_ref[shard, image], 0)
+        target = jnp.where((chip == shard) & (step < count), first + step, target)
+        first += count
+    slot = lax.broadcasted_iota(jnp.int32, (slots, places), 0)
+    unpack = jnp.where(slot == target, 1.0, 0.0).astype(BF16)
     for copy in copies:
         copy.wait()
     swaps = []
     totals = None
     for patch in range(own):
         landed = recv_buf[:, patch].reshape(shards * WINDOW, width)
-        incoming = jnp.dot(unpack_ref[...], landed, preferred_element_type=F32)
+        incoming = jnp.dot(unpack, landed, preferred_element_type=F32)
         normal, scale = norm_parts(layer_ref[patch].astype(F32))
         affine = normal * post_gain + post_bias
         rms = lax.rsqrt(row_mean(affine * affine) + EPSILON)
@@ -173,8 +197,11 @@
     sums_ref,
     units_ref,
     act_ref,
-    total_ref,
+    norm_ref,
+    unit_ref,
+    swap_out,
     swap_in,
+    normals,
     halves,
     half_in,
     seq_buf,
@@ -198,17 +225,21 @@
     dp_peers = others("dp", replicas)
     settle = greet([partner] + seq_peers + dp_peers)
     halves[...] = jnp.zeros_like(halves)
-    unit_rows = units_ref.shape[0]
+    width = act_ref.shape[2]
+    hidden = units_ref.shape[1]
+    spans = [(at, min(width, hidden - at)) for at in range(0, hidden, width)]
     halves[0, 0:1, :] = sums_ref[0:1, :]
     halves[0, 1:2, :] = sums_ref[1:2, :]
     halves[0, 2:3, :] = sums_ref[2:3, :]
     halves[1, 0:1, :] = sums_ref[3:4, :]
-    for index in range(unit_rows):
-        halves[core, 3 + index : 4 + index, :] = units_ref[index : index + 1, :]
+    for index, (at, size) in enumerate(spans):
+        halves[core, 3 + index : 4 + index, 0:size] = units_ref[:, at : at + size]
+    for patch in range(own):
+        swap_out[patch] = product_ref[other * own + patch].astype(BF16)
     settle()
     swaps = [
         remote(
-            product_ref.at[other * own + patch],
+            swap_out.at[patch],
             swap_in.at[patch],
             enc_send.at[patch],
             enc_recv.at[patch],
@@ -216,27 +247,39 @@
         )
         for patch in range(own)
     ]
-    pre_gain = pre_gain_ref[...]
+    pre_gain = pre_gain_ref[...].reshape(1, -1)
+    scales = []
+    for patch in range(own):
+        normal, scale = norm_parts(input_ref[core * own + patch].astype(F32))
+        normals[patch] = normal
+        scales.append(scale)
     gain_grad = None
     for patch in range(own):
-        normal, scale = norm_parts(input_ref[core * own + patch].astype(F32))
         swaps[patch].wait()
-        upstream = product_ref[core * own + patch, 0:slots, :] + swap_in[patch, 0:slots, :]
+        upstream = product_ref[core * own + patch, 0:slots, :] + swap_in[patch, 0:slots, :].astype(F32)
         parts = [
-            jnp.sum(upstream * normal, axis=0, keepdims=True),
+            jnp.sum(upstream * normals[patch], axis=0, keepdims=True),
             jnp.sum(upstream, axis=0, keepdims=True),
         ]
         gain_grad = parts if gain_grad is None else [a + b for a, b in zip(gain_grad, parts)]
-        act = res_ref[patch] + norm_pull(normal, scale, upstream * pre_gain)
-        act_ref[patch] = act.astype(BF16)
     halves[1, 1:2, :] = gain_grad[0]
     halves[1, 2:3, :] = gain_grad[1]
-    remote(halves.at[other], half_in, enc_send.at[own], enc_recv.at[own], partner).wait()
+
+    def finish(patch):
+        upstream = product_ref[core * own + patch, 0:slots, :] + swap_in[patch, 0:slots, :].astype(F32)
+        act = res_ref[patch] + norm_pull(normals[patch], scales[patch], upstream * pre_gain)
+        act_ref[patch] = act.astype(BF16)
+
+    half_copy = remote(halves.at[other], half_in, enc_send.at[own], enc_recv.at[own], partner)
+    finish(0)
+    half_copy.wait()
     seq_buf[me] = halves[core] + half_in[...]
     copies = [
         remote(seq_buf.at[me], seq_buf.at[me], seq_send.at[step], seq_recv.at[step], peer)
         for step, peer in enumerate(seq_peers)
     ]
+    for patch in range(1, own):
+        finish(patch)
     for copy in copies:
         copy.wait()
     total = seq_buf[0]
@@ -256,7 +299,10 @@
     remote(
         last_buf.at[core], last_buf.at[core], enc_send.at[own + 1], enc_recv.at[own + 1], partner
     ).wait()
-    total_ref[...] = last_buf[...]
+    for half in range(2):
+        norm_ref[3 * half : 3 * half + 3, :] = last_buf[half, 0:3, :]
+        for index, (at, size) in enumerate(spans):
+            unit_ref[half : half + 1, at : at + size] = last_buf[half, 3 + index : 4 + index, 0:size]
 
 
 def round_up(value, step):
@@ -279,7 +325,6 @@
     post_bias,
     merge_gain,
 ):
-    me = lax.axis_index("seq")
     shards = lax.axis_size("seq")
     replicas = lax.axis_size("dp")
     cores = lax.axis_size("enc")
@@ -289,28 +334,9 @@
     own, rows_dev, width = grad_rows.shape
     group, slots, _ = input_rows.shape
     padded = round_up(slots, WINDOW)
-    lengths, offsets, owners = image_tokens[0], image_offset[0], image_owner[0]
-
-    chips = jnp.arange(shards, dtype=jnp.int32)
-    steps = jnp.arange(WINDOW, dtype=jnp.int32)
-    my_images = lax.dynamic_slice_in_dim(jnp.stack([lengths, offsets, owners]), me, 1, 1)[:, 0]
-    to_chip = my_images[2][None, :] == chips[:, None]
-    sent_len = jnp.sum(jnp.where(to_chip, my_images[0][None, :], 0), axis=1)
-    sent_off = jnp.sum(jnp.where(to_chip, my_images[1][None, :], 0), axis=1)
-    source_row = jnp.where(
-        steps[None, :] < sent_len[:, None], sent_off[:, None] + steps[None, :], -1
-    ).reshape(-1)
-    pack = (source_row[:, None] == jnp.arange(rows_dev, dtype=jnp.int32)[None, :]).astype(BF16)
-    mine_len = jnp.sum(jnp.where(owners == me, lengths, 0), axis=1)
-    first = jnp.sum(jnp.where(chips[None, :] < chips[:, None], mine_len[None, :], 0), axis=1)
-    target_slot = jnp.where(
-        steps[None, :] < mine_len[:, None], first[:, None] + steps[None, :], -1
-    ).reshape(-1)
-    unpack = (jnp.arange(slots, dtype=jnp.int32)[:, None] == target_slot[None, :]).astype(BF16)
 
     vmem = pl.BlockSpec(memory_space=pltpu.VMEM)
     dma = pltpu.SemaphoreType.DMA
-    gain_row = pre_gain.reshape(1, width)
 
     def head_call(*refs):
         head_kernel(shards, *refs)
@@ -323,7 +349,7 @@
             jax.ShapeDtypeStruct((group, padded, width), BF16),
             jax.ShapeDtypeStruct((SUBLANES, width), F32),
         ),
-        in_specs=[vmem] * 10,
+        in_specs=[pl.BlockSpec(memory_space=pltpu.SMEM)] * 3 + [vmem] * 8,
         out_specs=(vmem,) * 4,
         scratch_shapes=[
             pltpu.VMEM((shards, own, WINDOW, width), BF16),
@@ -335,19 +361,23 @@
             dma((own,)),
             dma((own,)),
         ],
-        compiler_params=pltpu.CompilerParams(collective_id=0, has_side_effects=True),
+        compiler_params=pltpu.CompilerParams(
+            collective_id=0, has_side_effects=True, vmem_limit_bytes=HEAD_VMEM
+        ),
+        cost_estimate=pl.CostEstimate(flops=4_000_000_000, bytes_accessed=24_000_000, transcendentals=0),
         name="head",
     )(
-        pack,
-        unpack,
+        image_tokens[0],
+        image_offset[0],
+        image_owner[0],
         grad_rows,
         layer_rows,
         input_rows,
-        gain_row,
-        pre_bias.reshape(1, width),
-        post_gain.reshape(1, width),
-        post_bias.reshape(1, width),
-        merge_gain.reshape(1, width),
+        pre_gain,
+        pre_bias,
+        post_gain,
+        post_bias,
+        merge_gain,
     )
 
     pre_act = (
@@ -360,7 +390,7 @@
         preferred_element_type=F32,
     )
     hidden_grad = down_back * gelu_slope(pre_act)
-    fc1_part = jnp.sum(hidden_grad, axis=0)
+    units = jnp.sum(hidden_grad, axis=0, keepdims=True)
     hidden_units = fc1_bias.shape[0]
     product = lax.dot_general(
         hidden_grad.astype(BF16),
@@ -369,7 +399,6 @@
         preferred_element_type=F32,
     ).reshape(group, padded, width)
     unit_rows = round_up(hidden_units, width) // width
-    units = jnp.pad(fc1_part, (0, unit_rows * width - hidden_units)).reshape(unit_rows, width)
 
     grad_scale = 1.0 / math.sqrt(group * rows_dev * shards * replicas)
     sum_rows = round_up(3 + unit_rows, SUBLANES)
@@ -377,16 +406,19 @@
     def tail_call(*refs):
         tail_kernel(shards, replicas, grad_scale, *refs)
 
-    act_grad, totals = pl.pallas_call(
+    act_grad, norm_grads, unit_grads = pl.pallas_call(
         tail_call,
         out_shape=(
             jax.ShapeDtypeStruct((own, slots, width), BF16),
-            jax.ShapeDtypeStruct((cores, sum_rows, width), F32),
+            jax.ShapeDtypeStruct((6, width), F32),
+            jax.ShapeDtypeStruct((cores, hidden_units), F32),
         ),
         in_specs=[vmem] * 6,
-        out_specs=(vmem,) * 2,
+        out_specs=(vmem,) * 3,
         scratch_shapes=[
-            pltpu.VMEM((own, padded, width), F32),
+            pltpu.VMEM((own, padded, width), BF16),
+            pltpu.VMEM((own, padded, width), BF16),
+            pltpu.VMEM((own, slots, width), F32),
             pltpu.VMEM((cores, sum_rows, width), F32),
             pltpu.VMEM((sum_rows, width), F32),
             pltpu.VMEM((shards, sum_rows, width), F32),
@@ -401,10 +433,8 @@
         ],
         compiler_params=pltpu.CompilerParams(collective_id=1, has_side_effects=True),
         name="tail",
-    )(product, input_rows, gain_row, res_grad, sums, units)
-    norm_grads = totals[:, :3].reshape(-1, width)
-    fc1_grad = totals[:, 3 : 3 + unit_rows].reshape(cores, -1)[:, :hidden_units].reshape(-1)
-    return (act_grad[None], norm_grads, fc1_grad)
+    )(product, input_rows, pre_gain, res_grad, sums, units)
+    return (act_grad[None], norm_grads, unit_grads.reshape(-1))
 
 
 def solution(mesh):

time: 64 us -> 52.1 us (0.81)
  matrix products: 12.2 us -> 7.32 us
  other arithmetic: 3.25 us -> 0 us
  Pallas kernels: 31 us -> 28.5 us
  local copies, waits for them, and re-layouts: 16 us -> 14.8 us
    reshape x8 -> x1, local copies, waits for them, and re-layouts: 8.4 us -> 1.41 us  [body(): return (act_grad[None], norm_grads, unit_grads.reshape(-1))]
    unnamed x13 -> x34, local copies, waits for them, and re-layouts: 6.54 us -> 12.7 us
    dot_general x1, matrix products: 4.38 us -> 1.77 us  [body(): jnp.dot(normed.reshape(-1, width), fc1_weight, preferred_element_type=F32)]
    dot_general x1, matrix products: 5.13 us -> 2.78 us  [body(): lax.dot_general(hidden_grad.astype(BF16), fc1_weight, (((1,), (1,)), ((),...]
    pallas_call x1, Pallas kernels: 13 us -> 11 us  [body(): pl.pallas_call(head_call, out_shape=(jax.ShapeDtypeStruct((group, padded,...]
    convert_element_type x2 -> x0, other arithmetic: 1.29 us -> none  [the longest x1 0.68 us: body(): (source_row[:, None] == jnp.arange(rows_dev, dtype=jnp.int32)[None, :]).a...]
    reduce_sum x3 -> x0, other arithmetic: 1.08 us -> none  [the longest x1 0.82 us: body(): mine_len = jnp.sum(jnp.where(owners == me, lengths, 0), axis=1)]
    slice x2 -> x0, local copies, waits for them, and re-layouts: 0.89 us -> none  [the longest x1 0.89 us: body(): norm_grads = totals[:, :3].reshape(-1, width)]
where the time goes in v2:
time: 52.1 us; the launch traced here: 51.3 us
  Pallas kernels  28.5 us (55%)
  local copies, waits for them, and re-layouts  14.8 us (28%)
  matrix products  7.32 us (14%)
  between operations  0.75 us (1%)
    pallas_call x1, Pallas kernels, body(): pl.pallas_call(tail_call, out_shape=(jax.ShapeDtypeStruct((own, slots, wi...  17.5 us
    unnamed x34, local copies, waits for them, and re-layouts  12.7 us
    pallas_call x1, Pallas kernels, body(): pl.pallas_call(head_call, out_shape=(jax.ShapeDtypeStruct((group, padded,...  11 us
    dot_general x1, matrix products, body(): lax.dot_general(hidden_grad.astype(BF16), fc1_weight, (((1,), (1,)), ((),...  2.78 us
    dot_general x1, matrix products, body(): lax.dot_general(all_res.reshape(-1, width), fc2_weight, (((1,), (1,)), ((...  2.77 us
    dot_general x1, matrix products, body(): jnp.dot(normed.reshape(-1, width), fc1_weight, preferred_element_type=F32)  1.77 us
    reshape x1, local copies, waits for them, and re-layouts, body(): return (act_grad[None], norm_grads, unit_grads.reshape(-1))  1.41 us

profile of v2, /device:TPU:0, one launch (start us, length us, event | category | flops | bytes accessed | tf_op | source)
XLA Modules:
  0.0 51.3 jit_solution(17867264203184265957)
XLA Ops:
  0.6 1.0 %copy.23 = bf16[1,2,60,1152]{3,2,1,0:T(8,128)(2,1)S(1)} copy(bf16[1,2,60,1152]{3,1,2,0:T(2,128)(2,1)} %param.19) | data formatting | bytes 552960 | tf_op args[5]
  1.6 1.1 %copy.22 = bf16[1,4,60,1152]{3,2,1,0:T(8,128)(2,1)S(1)} copy(bf16[1,4,60,1152]{3,1,2,0:T(4,128)(2,1)} %param.18) | data formatting | bytes 1105920 | tf_op args[4]
  2.7 0.0 copy-start
  2.7 0.0 copy-start.3
  2.8 0.7 %copy-done.3 = f32[1152]{0:T(1024)S(1)} copy-done((f32[1152]{0:T(1024)S(1)}, f32[1152]{0:T(1024)}, u32[]{:S(2)}) %copy-start.3) | copy-done | bytes 4632
  3.5 0.0 copy-start.4
  3.5 0.9 %copy-done.4 = bf16[1,2,48,1152]{3,2,1,0:T(8,128)(2,1)S(1)} copy-done((bf16[1,2,48,1152]{3,2,1,0:T(8,128)(2,1)S(1)}, bf16[1,2,48,1152]{3,2,1,0:T(8,128)(2,1)}, u32[]{:S(2)}) %copy-start.4) | copy-done | bytes 221208
  4.4 0.0 copy-start.5
  4.4 0.7 %copy-done.5 = f32[1152]{0:T(1024)S(1)} copy-done((f32[1152]{0:T(1024)S(1)}, f32[1152]{0:T(1024)}, u32[]{:S(2)}) %copy-start.5) | copy-done | bytes 4632
  5.1 0.0 copy-start.6
  5.1 0.7 %copy-done.6 = f32[1152]{0:T(1024)S(1)} copy-done((f32[1152]{0:T(1024)S(1)}, f32[1152]{0:T(1024)}, u32[]{:S(2)}) %copy-start.6) | copy-done | bytes 4632
  5.8 0.0 copy-start.7
  5.8 0.7 %copy-done.7 = f32[1152]{0:T(1024)S(1)} copy-done((f32[1152]{0:T(1024)S(1)}, f32[1152]{0:T(1024)}, u32[]{:S(2)}) %copy-start.7) | copy-done | bytes 4632
  6.5 0.0 copy-start.8
  6.5 0.7 %copy-done.8 = f32[1152]{0:T(1024)S(1)} copy-done((f32[1152]{0:T(1024)S(1)}, f32[1152]{0:T(1024)}, u32[]{:S(2)}) %copy-start.8) | copy-done | bytes 4632
  7.2 0.0 copy-start.9
  7.2 0.7 %copy-done.9 = s32[1,4,4]{2,1,0:T(4,128)S(1)} copy-done((s32[1,4,4]{2,1,0:T(4,128)S(1)}, s32[1,4,4]{2,1,0:T(4,128)}, u32[]{:S(2)}) %copy-start.9) | copy-done | bytes 88
  7.9 0.0 copy-start.10
  7.9 0.7 %copy-done.10 = s32[1,4,4]{2,1,0:T(4,128)S(1)} copy-done((s32[1,4,4]{2,1,0:T(4,128)S(1)}, s32[1,4,4]{2,1,0:T(4,128)}, u32[]{:S(2)}) %copy-start.10) | copy-done | bytes 88
  8.6 0.0 copy-start.11
  8.6 0.7 %copy-done.11 = s32[1,4,4]{2,1,0:T(4,128)S(1)} copy-done((s32[1,4,4]{2,1,0:T(4,128)S(1)}, s32[1,4,4]{2,1,0:T(4,128)}, u32[]{:S(2)}) %copy-start.11) | copy-done | bytes 88
  9.2 0.0 copy-start.13
  9.2 0.0 copy-start.14
  9.2 11.0 %head.1 = (bf16[4,64,1152]{2,1,0:T(8,128)(2,1)S(1)}, f32[2,60,1152]{2,1,0:T(8,128)S(1)}, bf16[4,64,1152]{2,1,0:T(8,128)(2,1)S(1)}, f32[8,1152]{1,0:T(8,128)S(1)}) custom-call(s32[4,4]{1,0:T(4,128)S(1)} %bitcast.24, s32[4,4]{1,0:T(4,128)S(1)} %bitcast.25, s32[4,4]{1,0:T(4,128)S(1)} %bitcast.26, bf16[2,48,1152]{2,1,0:T(8,128)(2,1)S(1)} %bitcast.23, ...), custom_call_target="tpu_custom_call" | custom-call | flops 4000000000 | bytes 24000000 | tf_op jit(solution)/shard_map/head/pallas_call | solution.py:344
  20.3 0.0 copy-done
  20.3 0.0 copy-start.1
  20.3 0.0 copy-start.2
  20.3 0.0 copy-done.13
  20.3 0.0 copy-done.14
  20.3 0.0 copy-start.12
  20.4 1.8 %convolution_add_fusion = f32[256,2152]{0,1:T(8,128)S(1)} fusion(bf16[256,1152]{1,0:T(8,128)(2,1)S(1)} %bitcast.28, bf16[1152,2152]{0,1:T(8,128)(2,1)S(1)} %copy-done.13, f32[2152]{0:T(1024)S(1)} %copy-done.14), kind=kOutput, calls=%fused_computation.1 | convolution fusion | flops 1269852160 | bytes 7760288 | tf_op jit(solution)/shard_map/dot_general | solution.py:384
  22.1 0.0 copy-done.1
  22.1 0.0 copy-done.2
  22.2 0.8 %copy-done.12 = bf16[2152,1152]{1,0:T(8,128)(2,1)S(1)} copy-done((bf16[2152,1152]{1,0:T(8,128)(2,1)S(1)}, bf16[2152,1152]{1,0:T(8,128)(2,1)}, u32[]{:S(2)}) %copy-start.12) | copy-done | bytes 4958232
  23.0 2.8 %fusion.7 = (f32[2152]{0:T(1024)S(1)}, bf16[256,2152]{0,1:T(8,128)(2,1)S(1)}) fusion(f32[256,2152]{0,1:T(8,128)S(1)} %convolution_add_fusion, bf16[256,1152]{1,0:T(8,128)(2,1)S(1)} %bitcast.27, bf16[2152,1152]{1,0:T(8,128)(2,1)S(1)} %copy-done.12), kind=kOutput, calls=%fused_computation.13 | convolution fusion | flops 1280317312 | bytes 8862112 | tf_op jit(solution)/shard_map/dot_general | solution.py:386
  25.7 0.6 %broadcast_in_dim.7.refs_5_ = f32[1,2152]{1,0:T(1,128)} reshape(f32[2152]{0:T(1024)S(1)} %get-tuple-element.20) | data formatting | bytes 17216 | tf_op jit(solution)/shard_map/broadcast_in_dim | solution.py:393
  26.3 2.8 %fusion.5 = f32[256,1152]{1,0:T(8,128)} fusion(bf16[1152,2152]{0,1:T(8,128)(2,1)S(1)} %copy-done.13, bf16[256,2152]{0,1:T(8,128)(2,1)S(1)} %get-tuple-element.21), kind=kOutput, calls=%fused_computation.9 | convolution fusion | flops 1269301248 | bytes 7239680 | tf_op jit(solution)/shard_map/dot_general | solution.py:395
  29.1 17.5 %tail.1 = (bf16[2,60,1152]{2,1,0:T(8,128)(2,1)}, f32[6,1152]{1,0:T(8,128)}, f32[2,2152]{1,0:T(2,128)}) custom-call(f32[4,64,1152]{2,1,0:T(8,128)} %bitcast.29, bf16[4,60,1152]{2,1,0:T(8,128)(2,1)} %bitcast.21, f32[1152]{0:T(1024)} %refs_2_.1, f32[2,60,1152]{2,1,0:T(8,128)} %copy-done.1, f32[8,1152]{1,0:T(8,128)} %copy-done.2, f32[1,2152]{1,0:T(1,128)} %broadcast_in_dim.7.refs_5_), custom_call_target="tpu_custom_call" | custom-call | tf_op jit(solution)/shard_map/tail/pallas_call | solution.py:409
  46.6 2.0 %copy.19 = bf16[1,2,60,1152]{3,1,2,0:T(2,128)(2,1)} copy(bf16[1,2,60,1152]{3,2,1,0:T(8,128)(2,1)} %bitcast.30) | data formatting | bytes 552960
  48.5 1.4 %reshape.22 = f32[4304]{0:T(1024)} reshape(f32[2,2152]{1,0:T(2,128)} %get-tuple-element.16) | data formatting | bytes 34432 | tf_op jit(solution)/shard_map/reshape | solution.py:437
  49.9 1.4 %copy.25 = f32[6,1152]{1,0:T(8,128)} copy(f32[6,1152]{1,0:T(8,128)} %get-tuple-element.28) | data formatting | bytes 55296
Async XLA Ops:
  2.7 17.6 %copy-start = (bf16[1,4,60,1152]{3,2,1,0:T(8,128)(2,1)}, bf16[1,4,60,1152]{3,2,1,0:T(8,128)(2,1)S(1)}, u32[]{:S(2)}) copy-start(bf16[1,4,60,1152]{3,2,1,0:T(8,128)(2,1)S(1)} %copy.22) | copy-start | bytes 1658884
  2.7 0.7 %copy-start.3 = (f32[1152]{0:T(1024)S(1)}, f32[1152]{0:T(1024)}, u32[]{:S(2)}) copy-start(f32[1152]{0:T(1024)} %refs_2_.1) | copy-start | bytes 13828
  3.5 0.9 %copy-start.4 = (bf16[1,2,48,1152]{3,2,1,0:T(8,128)(2,1)S(1)}, bf16[1,2,48,1152]{3,2,1,0:T(8,128)(2,1)}, u32[]{:S(2)}) copy-start(bf16[1,2,48,1152]{3,2,1,0:T(8,128)(2,1)} %param.14) | copy-start | bytes 663556
  4.4 0.7 %copy-start.5 = (f32[1152]{0:T(1024)S(1)}, f32[1152]{0:T(1024)}, u32[]{:S(2)}) copy-start(f32[1152]{0:T(1024)} %refs_7_.1) | copy-start | bytes 13828
  5.1 0.7 %copy-start.6 = (f32[1152]{0:T(1024)S(1)}, f32[1152]{0:T(1024)}, u32[]{:S(2)}) copy-start(f32[1152]{0:T(1024)} %refs_8_.1) | copy-start | bytes 13828
  5.8 0.7 %copy-start.7 = (f32[1152]{0:T(1024)S(1)}, f32[1152]{0:T(1024)}, u32[]{:S(2)}) copy-start(f32[1152]{0:T(1024)} %refs_9_.1) | copy-start | bytes 13828
  6.5 0.7 %copy-start.8 = (f32[1152]{0:T(1024)S(1)}, f32[1152]{0:T(1024)}, u32[]{:S(2)}) copy-start(f32[1152]{0:T(1024)} %refs_10_.1) | copy-start | bytes 13828
  7.2 0.7 %copy-start.9 = (s32[1,4,4]{2,1,0:T(4,128)S(1)}, s32[1,4,4]{2,1,0:T(4,128)}, u32[]{:S(2)}) copy-start(s32[1,4,4]{2,1,0:T(4,128)} %param.15) | copy-start | bytes 196
  7.9 0.7 %copy-start.10 = (s32[1,4,4]{2,1,0:T(4,128)S(1)}, s32[1,4,4]{2,1,0:T(4,128)}, u32[]{:S(2)}) copy-start(s32[1,4,4]{2,1,0:T(4,128)} %param.16) | copy-start | bytes 196
  8.6 0.7 %copy-start.11 = (s32[1,4,4]{2,1,0:T(4,128)S(1)}, s32[1,4,4]{2,1,0:T(4,128)}, u32[]{:S(2)}) copy-start(s32[1,4,4]{2,1,0:T(4,128)} %param.17) | copy-start | bytes 196
  9.2 11.1 %copy-start.13 = (bf16[1152,2152]{0,1:T(8,128)(2,1)S(1)}, bf16[1152,2152]{0,1:T(8,128)(2,1)}, u32[]{:S(2)}) copy-start(bf16[1152,2152]{0,1:T(8,128)(2,1)} %param.22) | copy-start | bytes 14874628
  9.2 11.1 %copy-start.14 = (f32[2152]{0:T(1024)S(1)}, f32[2152]{0:T(1024)}, u32[]{:S(2)}) copy-start(f32[2152]{0:T(1024)} %param.23) | copy-start | bytes 25828
  20.3 1.8 %copy-start.1 = (f32[2,60,1152]{2,1,0:T(8,128)}, f32[2,60,1152]{2,1,0:T(8,128)S(1)}, u32[]{:S(2)}) copy-start(f32[2,60,1152]{2,1,0:T(8,128)S(1)} %get-tuple-element.12.refs_3_) | copy-start | bytes 1658884
  20.3 1.8 %copy-start.2 = (f32[8,1152]{1,0:T(8,128)}, f32[8,1152]{1,0:T(8,128)S(1)}, u32[]{:S(2)}) copy-start(f32[8,1152]{1,0:T(8,128)S(1)} %get-tuple-element.13.refs_4_) | copy-start | bytes 110596
  20.3 2.6 %copy-start.12 = (bf16[2152,1152]{1,0:T(8,128)(2,1)S(1)}, bf16[2152,1152]{1,0:T(8,128)(2,1)}, u32[]{:S(2)}) copy-start(bf16[2152,1152]{1,0:T(8,128)(2,1)} %param.24) | copy-start | bytes 14874628
